TPU v7x, 256 devices: a whole 4x4x8 slice. The times are simulated.
256 devices in a mesh: pair: 8 (over y, x_hi), mode: 32 (over z, x_lo, core).
Axes of the slice: x: 4 (x_hi: 2, x_lo: 2; x = x_hi * 2 + x_lo), y: 4, z: 8, core: 2. Of those that a mesh axis runs over, the one named last changes fastest.
Arguments:
- phi: bfloat16 [8, 384, 384, 384], P('pair', 'mode'), may hold values from -6 to 6
- eigvecs: bfloat16 [12, 384, 384], replicated, may hold values from -0.3125 to 0.3125
- freqs: float32 [12, 384], replicated, may hold values from 0.5 to 8
- occupations: float32 [12, 384], replicated, may hold values from 0.02 to 4
- smearing: float32 [12, 384], replicated, may hold values from 0.2 to 1
- probes: float32 [8, 2], P('pair'), may hold values from 0.5 to 8
- pair_index: int32 [8, 3], P('pair'), may hold values from 0 to 11
Outputs:
- sigma: float32 [384, 2, 384], P('mode', None, 'pair')
All inputs are finite; a program needn't handle non-finite values.
Results may differ from a plain program's by a relative error of at most 0.0013.
Values may be sent and summed in bfloat16 or wider, within the bound.
A program may use at most 64 MiB of HBM per device.

v0:
```python
import math

import jax
import jax.numpy as jnp
from jax import lax
from jax.sharding import PartitionSpec as P


def lorentz(offset, eta):
    return eta / (offset * offset + eta * eta)


def weights(f_one, n_one, h_one, f_two, n_two, h_two, omegas):
    total = f_two[:, None] + f_one[None, :]
    differ = f_two[:, None] - f_one[None, :]
    eta = 0.5 * (h_two[:, None] + h_one[None, :])
    bose_sum = 1.0 + n_one[None, :] + n_two[:, None]
    bose_diff = n_one[None, :] - n_two[:, None]
    result = []
    for probe in range(2):
        omega = omegas[probe]
        value = bose_sum * (lorentz(omega - total, eta) - lorentz(omega + total, eta))
        value = value + bose_diff * (lorentz(omega - differ, eta) - lorentz(omega + differ, eta))
        result.append(value)
    return jnp.stack(result)


def shards(phi, eigvecs, freqs, occupations, smearing, probes, pair_index):
    tensor = phi[0]
    slices = tensor.shape[0]
    modes = tensor.shape[1]
    q_one = pair_index[0, 0]
    q_two = pair_index[0, 1]
    q_three = pair_index[0, 2]
    e_one = lax.dynamic_index_in_dim(eigvecs, q_one, 0, keepdims=False)
    e_two = lax.dynamic_index_in_dim(eigvecs, q_two, 0, keepdims=False)
    e_three = lax.dynamic_index_in_dim(eigvecs, q_three, 0, keepdims=False)
    first = jnp.dot(
        tensor.reshape(slices * modes, modes), e_one, preferred_element_type=jnp.float32
    )
    first = first.astype(jnp.bfloat16).reshape(slices, modes, modes)
    second = jnp.einsum("cbi,bj->cji", first, e_two, preferred_element_type=jnp.float32).astype(
        jnp.bfloat16
    )
    arrived = lax.all_to_all(second, "mode", split_axis=1, concat_axis=0, tiled=True)
    span = arrived.shape[1]
    count = arrived.shape[2]
    flat = lax.dot_general(
        e_three,
        arrived.reshape(arrived.shape[0], span * count),
        (((0,), (0,)), ((), ())),
        preferred_element_type=jnp.float32,
    )
    rotated = flat.astype(jnp.bfloat16).reshape(modes, span, count)
    span = rotated.shape[1]
    offset = lax.axis_index("mode") * span
    f_two = lax.dynamic_slice_in_dim(freqs[q_two], offset, span)
    n_two = lax.dynamic_slice_in_dim(occupations[q_two], offset, span)
    h_two = lax.dynamic_slice_in_dim(smearing[q_two], offset, span)
    wgt = weights(freqs[q_one], occupations[q_one], smearing[q_one], f_two, n_two, h_two, probes[0])
    flat_rot = rotated.reshape(modes, span * modes)
    weighted = (wgt.reshape(2, 1, span * modes) * flat_rot.astype(jnp.float32)[None]).astype(
        jnp.bfloat16
    )
    pair_size = lax.axis_size("pair")
    partial_rows = lax.psum_scatter(
        jnp.einsum("wkl,nl->kwn", weighted, flat_rot, preferred_element_type=jnp.float32),
        "mode",
        scatter_dimension=0,
        tiled=True,
    )
    local = lax.psum_scatter(partial_rows, "pair", scatter_dimension=2, tiled=True)
    row_count = local.shape[0]
    col_count = local.shape[2]
    row_ids = lax.axis_index("mode") * row_count + jnp.arange(row_count, dtype=jnp.int32)
    col_ids = lax.axis_index("pair") * col_count + jnp.arange(col_count, dtype=jnp.int32)
    offdiag = (row_ids[:, None] != col_ids[None, :]).astype(jnp.float32)
    scale = 1.0 / (modes * math.sqrt(pair_size))
    return local * offdiag[:, None, :] * scale


def solution(mesh):
    return jax.shard_map(
        shards,
        mesh=mesh,
        in_specs=(
            P("pair", "mode", None, None),
            P(),
            P(),
            P(),
            P(),
            P("pair", None),
            P("pair", None),
        ),
        out_specs=P("mode", None, "pair"),
        check_vma=False,
    )
```

profile of v0, /device:TPU:8, one launch (start us, length us, event | category | flops | bytes accessed | tf_op | source)
XLA Modules:
  0.0 480.9 jit_solution(6054120458659135044)
XLA Ops:
  6.5 0.0 copy-start
  6.5 1.4 fusion.20
  11.0 0.0 copy-done
  11.0 5.9 %fusion.3 = bf16[4608,384]{0,1:T(8,128)(2,1)} fusion(bf16[4608,384]{1,0:T(8,128)(2,1)} %bitcast.63, bf16[12,384,384]{2,1,0:T(8,128)(2,1)S(1)} %copy-done, s32[]{:T(128)S(6)} %select_n.27), kind=kOutput, calls=%fused_computation.6 | convolution fusion | flops 1360723968 | bytes 7372804 | tf_op jit(solution)/shard_map/dot_general | solution.py:38
  16.9 5.7 %copy.22 = bf16[4608,384]{1,0:T(8,128)(2,1)} copy(bf16[4608,384]{0,1:T(8,128)(2,1)} %fusion.3) | data formatting | bytes 7077888 | tf_op jit(solution)/shard_map/convert_element_type | solution.py:41
  23.2 4.0 convert_bitcast_fusion
  27.2 4.4 copy.23
  31.7 0.0 copy-start.2
  31.7 10.0 %all-to-all-start = ((bf16[12,384,384]{2,0,1:T(8,128)(2,1)}), bf16[12,384,384]{2,0,1:T(8,128)(2,1)}, u32[]{:S(2)}, u32[]{:S(2)}) async-start(bf16[12,384,384]{2,0,1:T(8,128)(2,1)} %copy.23), calls=%async_computation | async-start | bytes 9437184 | tf_op jit(solution)/shard_map/all_to_all | solution.py:45
  41.7 0.2 all-reduce.3.cloned.1.call-start
  43.2 0.8 dynamic-slice_bitcast_fusion
  44.0 0.7 add.329
  44.7 1.4 add.330
  46.1 0.7 dynamic-slice_reduce_fusion
  46.8 0.6 add.332
  47.4 1.4 add.333
  48.8 0.7 add_reduce_fusion
  49.5 0.6 sub.150
  50.1 1.4 sub.151
  51.5 0.8 dynamic-slice_bitcast_fusion.2
  52.2 0.7 add.320
  52.9 1.4 add.321
  54.3 0.6 add.317
  54.9 1.4 add.318
  56.2 0.7 add.323
  56.9 1.4 add.324
  58.2 0.6 add.326
  58.8 1.4 add.327
  60.2 0.0 copy-done.2
  60.2 0.7 fusion.19
  60.9 2.4 multiply_add_fusion.1
  63.3 0.6 copy.34
  64.6 82.5 %all-to-all-done = bf16[12,384,384]{2,0,1:T(8,128)(2,1)} async-done(((bf16[12,384,384]{2,0,1:T(8,128)(2,1)}), bf16[12,384,384]{2,0,1:T(8,128)(2,1)}, u32[]{:S(2)}, u32[]{:S(2)}) %all-to-all-start) | async-done | bytes 3538976 | tf_op jit(solution)/shard_map/all_to_all | solution.py:45
  147.1 3.5 copy.25
  150.6 1.1 copy.32
  151.6 0.0 copy-start.1
  151.6 2.1 fusion.21
  153.7 0.0 copy-done.1
  153.7 3.9 fusion.5
  157.7 0.0 copy-start.3
  157.7 3.4 copy.26
  161.1 0.0 all-reduce.3.cloned.1.call-update
  161.1 0.0 reduce-scatter.4.cloned.1.call-start
  161.2 0.0 copy-done.3
  161.2 0.6 dynamic-slice.3
  162.4 223.0 %all-reduce.3.cloned.1.call-done = f32[384,2,384]{2,1,0:T(2,128)} async-done(((f32[384,2,384]{2,1,0:T(2,128)}), f32[384,2,384]{2,1,0:T(2,128)}) %all-reduce.3.cloned.1.call-update) | async-done | bytes 1179664
  385.4 1.4 constant_dynamic-slice_fusion.1
  386.8 2.9 copy.29
  389.8 3.4 reshape.437
  393.1 0.0 reduce-scatter.4.cloned.1.call-update
  393.1 0.7 compare_convert_fusion
  393.8 76.1 %reduce-scatter.4.cloned.1.call-done = f32[48,24]{1,0:T(8,128)} async-done(((f32[384,24]{1,0:T(8,128)}), f32[48,24]{1,0:T(8,128)}) %reduce-scatter.4.cloned.1.call-update) | async-done | bytes 4624
  469.9 1.7 reshape.438
  471.5 1.2 copy.30
  472.7 1.3 multiply_multiply_fusion
  (3 shorter events, 0.0 us)
Async XLA Ops:
  6.5 4.5 copy-start
  31.7 28.5 %copy-start.2 = (f32[1,2]{1,0:T(1,128)S(1)}, f32[1,2]{1,0:T(1,128)}, u32[]{:S(2)}) copy-start(f32[1,2]{1,0:T(1,128)} %param.12) | copy-start | bytes 28
  31.7 115.4 %all-to-all-start = ((bf16[12,384,384]{2,0,1:T(8,128)(2,1)}), bf16[12,384,384]{2,0,1:T(8,128)(2,1)}, u32[]{:S(2)}, u32[]{:S(2)}) async-start(bf16[12,384,384]{2,0,1:T(8,128)(2,1)} %copy.23), calls=%async_computation | async-start | bytes 9437184 | tf_op jit(solution)/shard_map/all_to_all | solution.py:45
  41.7 343.7 %all-reduce.3.cloned.1.call-start = ((), (), s32[]{:S(2)}) async-start(), calls=%async_computation.3 | async-start | bytes 2359296
  151.6 2.1 copy-start.1
  157.7 3.5 copy-start.3
  161.1 308.8 %reduce-scatter.4.cloned.1.call-start = ((), (), s32[]{:S(2)}) async-start(), calls=%async_computation.2 | async-start | bytes 221184
Sparse Core Ops, SparseCore 0:
  161.2 224.1 all-reduce.2
  393.3 76.5 reduce-scatter.3
where the time goes:
time: 482 us; the launch traced here: 481 us
  waiting for transfers between devices  382 us (79%)
  local copies, waits for them, and re-layouts  48.2 us (10%)
  between operations  19.8 us (4%)
  matrix products  15.9 us (3%)
  starting transfers between devices  10.3 us (2%)
  other arithmetic  5.15 us (1%)
    unnamed x4, waiting for transfers between devices  299 us
    all_to_all x1, waiting for transfers between devices, shards(): lax.all_to_all(second, 'mode', split_axis=1, concat_axis=0, tiled=True)  82.5 us
    unnamed x16, local copies, waits for them, and re-layouts  12.8 us
    all_to_all x1, starting transfers between devices, shards(): lax.all_to_all(second, 'mode', split_axis=1, concat_axis=0, tiled=True)  10 us
  transfers between devices with their start and end apart: 3, of which 3 were waited for; matrix products, arithmetic and copies ran while one was open for 5% of the time, Pallas kernels for 0%

commit v1 on v0

v1 whole, which is shorter than its diff:
```python
import math

import jax
import jax.numpy as jnp
import numpy as np
from jax import lax
from jax.experimental import pallas as pl
from jax.experimental.pallas import tpu as pltpu
from jax.sharding import PartitionSpec as P

MESH = pl.DeviceIdType.MESH
F32 = jnp.float32
BF16 = jnp.bfloat16

M = 384
Z = 8
G = 4
L = 128
NB = M // L
B = M // (Z * G)
ROWS = B * B
PEERS = Z * G - 1
PAIRS = 8
PLANE = 15


def lorentz(offset, eta):
    return eta / (offset * offset + eta * eta)


def dot(a, b, dims=((1,), (0,))):
    return lax.dot_general(a, b, (dims, ((), ())), preferred_element_type=F32)


def kernel(
    pidx, probes, phi, eig, freqs, occ, smear, perm, out,
    e_two_t, e_one, e_three_t, u_f, u_b, send, recv, wgt, acc, half_own, half_got, plane_src,
    plane_got, turned, z_got,
    a_send, a_recv, c_send, c_recv, p_send, p_recv, z_send, z_recv, local,
):
    mode = lax.axis_index("mode")
    pair = lax.axis_index("pair")
    z = mode // G
    g = lax.rem(mode, G)
    xl = g // 2
    core = lax.rem(g, 2)
    y = pair // 2
    xh = lax.rem(pair, 2)

    def mate(e):
        return lax.rem(xl + e // 2, 2) * 2 + lax.rem(core + e % 2, 2)

    def plane_peer(d):
        return lax.rem(y + d // 4, 4), lax.rem(xh + (d // 2) % 2, 2), lax.rem(xl + d % 2, 2)

    def plane_back(d):
        return lax.rem(y + 4 - d // 4, 4), lax.rem(xh + (d // 2) % 2, 2), lax.rem(xl + d % 2, 2)

    barrier = pltpu.get_barrier_semaphore()

    def greet(i, carry):
        other = lax.rem(mode + 1 + i, Z * G)
        pl.semaphore_signal(barrier, inc=1, device_id=(pair, other), device_id_type=MESH)
        return carry

    lax.fori_loop(0, PEERS, greet, 0)
    for d in range(2, PLANE + 1):
        yy, hh, ll = plane_back(d)
        pl.semaphore_signal(
            barrier, inc=1, device_id=(yy * 2 + hh, z * G + ll * 2 + core), device_id_type=MESH
        )

    q_one = pidx[0, 0]
    q_two = pidx[0, 1]
    q_three = pidx[0, 2]
    rows_i = lax.broadcasted_iota(jnp.int32, (M, M), 0)
    cols_i = lax.broadcasted_iota(jnp.int32, (M, M), 1)
    eye = (rows_i == cols_i).astype(F32).astype(BF16)
    e_two_t[...] = dot(eye, eig[q_two], ((1,), (1,))).astype(BF16)
    e_three_t[...] = dot(perm[...], eig[q_three], ((1,), (1,))).astype(BF16)
    e_one[...] = eig[q_one]

    def rotate_two(c, carry):
        rows = dot(e_two_t[...], phi[0, c])
        for b in range(NB):
            u_f[b, pl.ds(c, M, stride=B), :] = rows[:, b * L : (b + 1) * L]
        return carry

    lax.fori_loop(0, B, rotate_two, 0)

    def ship(chunk, peer, zz, gg):
        return pltpu.make_async_remote_copy(
            src_ref=send.at[chunk, zz * G + gg],
            dst_ref=recv.at[chunk, :, pl.ds(3 * mode, 3)],
            send_sem=a_send.at[chunk, peer],
            recv_sem=a_recv.at[chunk, peer],
            device_id=(pair, zz * G + gg),
            device_id_type=MESH,
        )

    def keep(chunk):
        return pltpu.make_async_copy(
            send.at[chunk, mode], recv.at[chunk, :, pl.ds(3 * mode, 3)], local.at[chunk]
        )

    def far(t):
        h = (t + 1) // 2
        return lax.rem(z + 4 + (1 - 2 * lax.rem(t, 2)) * h, Z)

    def first_chunk(zz):
        start = pl.multiple_of(zz * (G * ROWS), G * ROWS)
        rows = jnp.concatenate(
            [u_f[b, pl.ds(start, G * ROWS), :] for b in range(NB)], axis=1
        ).astype(BF16)
        u_b[pl.ds(start, G * ROWS), :] = rows
        done = dot(rows, e_one[:, :L]).astype(BF16)
        send.at[0, pl.ds(zz * G, G)].reshape(G * ROWS, L)[...] = done

    def later_chunks(zz):
        start = pl.multiple_of(zz * (G * ROWS), G * ROWS)
        done = dot(u_b[pl.ds(start, G * ROWS), :], e_one[:, L:]).astype(BF16)
        for chunk in range(1, NB):
            send.at[chunk, pl.ds(zz * G, G)].reshape(G * ROWS, L)[...] = done[
                :, (chunk - 1) * L : chunk * L
            ]

    def ship_all(chunk, t):
        zz = far(t)
        for e in range(G):
            ship(chunk, t * G + e, zz, mate(e)).start()

    def ship_near(chunk):
        for e in range(1, G):
            ship(chunk, (Z - 1) * G + e - 1, z, mate(e)).start()
        keep(chunk).start()

    first_chunk(far(0))
    pl.semaphore_wait(barrier, PEERS + PLANE - 1)
    ship_all(0, 0)

    def step_first(t, carry):
        first_chunk(far(t))
        ship_all(0, t)
        return carry

    lax.fori_loop(1, Z - 1, step_first, 0)
    first_chunk(z)
    ship_near(0)

    def step_later(t, carry):
        later_chunks(far(t))
        ship_all(1, t)
        return carry

    lax.fori_loop(0, Z - 1, step_later, 0)
    later_chunks(z)
    ship_near(1)

    def step_last(t, carry):
        ship_all(2, t)
        return carry

    lax.fori_loop(0, Z - 1, step_last, 0)
    ship_near(2)

    lane = lax.broadcasted_iota(jnp.int32, (B, M), 1)
    mine = lane == mode * B + lax.broadcasted_iota(jnp.int32, (B, M), 0)

    def column(table):
        return jnp.sum(jnp.where(mine, table[pl.ds(q_two, 1), :], 0.0), axis=1, keepdims=True)

    f_one = freqs[pl.ds(q_one, 1), :]
    n_one = occ[pl.ds(q_one, 1), :]
    h_one = smear[pl.ds(q_one, 1), :]
    f_two = column(freqs)
    n_two = column(occ)
    h_two = column(smear)
    total = f_two + f_one
    differ = f_two - f_one
    eta = 0.5 * (h_two + h_one)
    bose_sum = 1.0 + n_one + n_two
    bose_diff = n_one - n_two
    for w in range(2):
        omega = probes[0, w]
        value = bose_sum * (lorentz(omega - total, eta) - lorentz(omega + total, eta))
        value = value + bose_diff * (lorentz(omega - differ, eta) - lorentz(omega + differ, eta))
        for j in range(B):
            wgt[w, j] = value[j : j + 1, :]

    acc[...] = jnp.zeros_like(acc)
    span = M // G

    def take(chunk):
        def wait_one(i, carry):
            ship(chunk, i, z, mate(1)).wait_recv()
            return carry

        lax.fori_loop(0, PEERS, wait_one, 0)
        keep(chunk).wait()

        def gram(jp, carry):
            block = jnp.concatenate(
                [recv.at[chunk, 2 * jp + s].reshape(M, L)[...] for s in range(2)], axis=1
            )
            rot = dot(e_three_t[...], block).astype(BF16)
            hole = jnp.zeros((L - span, 2 * L), BF16)
            parts = []
            for k in range(G):
                parts += [rot[k * span : (k + 1) * span], hole]
            right = jnp.concatenate(parts, axis=0)
            wide = rot.astype(F32)
            for w in range(2):
                row = jnp.concatenate(
                    [wgt[w, 2 * jp + s, :, chunk * L : (chunk + 1) * L] for s in range(2)],
                    axis=1,
                )
                part = dot((wide * row).astype(BF16), right, ((1,), (1,)))
                for k in range(G):
                    acc[k, w * M : (w + 1) * M, :] += part[:, k * L : (k + 1) * L]
            return carry

        lax.fori_loop(0, B // 2, gram, 0)

    for chunk in range(NB):
        take(chunk)

    for s in range(2):
        half_own.at[s].reshape(2 * M, L)[...] = acc[2 * s + 1 - core].astype(BF16)
    swaps = []
    for s in range(2):
        swap = pltpu.make_async_remote_copy(
            src_ref=half_own.at[s],
            dst_ref=half_got.at[s],
            send_sem=c_send.at[s],
            recv_sem=c_recv.at[s],
            device_id=(pair, z * G + xl * 2 + 1 - core),
            device_id_type=MESH,
        )
        swap.start()
        swaps.append(swap)
    for s in range(2):
        swaps[s].wait_recv()
        both = acc[2 * s + core] + half_got.at[s].reshape(2 * M, L)[...].astype(F32)
        plane_src.at[s].reshape(2 * M, L)[...] = both.astype(BF16)

    hops = []
    for d in range(1, PLANE + 1):
        yy, hh, ll = plane_peer(d)
        hop = pltpu.make_async_remote_copy(
            src_ref=plane_src.at[ll, :, :, yy * 2 + hh],
            dst_ref=plane_got.at[d],
            send_sem=p_send.at[d - 1],
            recv_sem=p_recv.at[d - 1],
            device_id=(yy * 2 + hh, z * G + ll * 2 + core),
            device_id_type=MESH,
        )
        hop.start()
        hops.append(hop)
    wide_rows = 2 * M // PAIRS
    kept = pltpu.make_async_copy(plane_src.at[xl, :, :, pair], plane_got.at[0], local.at[NB])
    kept.start()
    kept.wait()
    for hop in hops:
        hop.wait_recv()
    whole = plane_got.at[0].reshape(wide_rows, L)[...].astype(F32)
    for d in range(1, PLANE + 1):
        whole = whole + plane_got.at[d].reshape(wide_rows, L)[...].astype(F32)

    square = jnp.concatenate([whole, jnp.zeros((L - wide_rows, L), F32)], axis=0)
    turned.reshape(L, L)[...] = square.T
    rises = []
    for d in range(1, Z):
        zz = lax.rem(z + d, Z)
        rise = pltpu.make_async_remote_copy(
            src_ref=turned.at[pl.ds(3 * zz, 3)],
            dst_ref=z_got.at[d],
            send_sem=z_send.at[d - 1],
            recv_sem=z_recv.at[d - 1],
            device_id=(pair, zz * G + g),
            device_id_type=MESH,
        )
        rise.start()
        rises.append(rise)
    stay = pltpu.make_async_copy(turned.at[pl.ds(3 * z, 3)], z_got.at[0], local.at[NB + 1])
    stay.start()
    stay.wait()
    for rise in rises:
        rise.wait_recv()
    result = z_got.at[0].reshape(B, L)[...]
    for d in range(1, Z):
        result = result + z_got.at[d].reshape(B, L)[...]

    cols = M // PAIRS
    row_id = mode * B + lax.broadcasted_iota(jnp.int32, (B, cols), 0)
    col_id = pair * cols + lax.broadcasted_iota(jnp.int32, (B, cols), 1)
    scale = 1.0 / (M * math.sqrt(PAIRS))
    for w in range(2):
        out[:, w, :] = jnp.where(row_id == col_id, 0.0, result[:, w * cols : (w + 1) * cols] * scale)

    def sent(i, carry):
        for chunk in range(NB):
            ship(chunk, i, z, mate(1)).wait_send()
        return carry

    lax.fori_loop(0, PEERS, sent, 0)
    for copy in swaps + hops + rises:
        copy.wait_send()


def shards(phi, eigvecs, freqs, occupations, smearing, probes, pair_index):
    k = np.arange(M)
    natural = (k % (M // G)) // B * (G * B) + k // (M // G) * B + k % B
    perm = jnp.asarray(np.equal(natural[:, None], k[None, :]), BF16)
    vmem = pl.BlockSpec(memory_space=pltpu.VMEM)
    smem = pl.BlockSpec(memory_space=pltpu.SMEM)
    dma = pltpu.SemaphoreType.DMA
    return pl.pallas_call(
        kernel,
        out_shape=jax.ShapeDtypeStruct((B, 2, M // PAIRS), F32),
        in_specs=[smem, smem] + [vmem] * 6,
        out_specs=vmem,
        scratch_shapes=[
            pltpu.VMEM((M, M), BF16),
            pltpu.VMEM((M, M), BF16),
            pltpu.VMEM((M, M), BF16),
            pltpu.VMEM((NB, M * B, L), F32),
            pltpu.VMEM((M * B, M), BF16),
            pltpu.VMEM((NB, Z * G, B, 3, 4, L), BF16),
            pltpu.VMEM((NB, B, M // 4, 4, L), BF16),
            pltpu.VMEM((2, B, 1, M), F32),
            pltpu.VMEM((G, 2 * M, L), F32),
            pltpu.VMEM((2, 2 * M // 4, 4, L), BF16),
            pltpu.VMEM((2, 2 * M // 4, 4, L), BF16),
            pltpu.VMEM((2, 2, G, Z, 3, 4, L), BF16),
            pltpu.VMEM((PLANE + 1, 2, G, 3, 4, L), BF16),
            pltpu.VMEM((L // 4, 4, L), F32),
            pltpu.VMEM((Z, 3, 4, L), F32),
            dma((NB, PEERS)),
            dma((NB, PEERS)),
            dma((2,)),
            dma((2,)),
            dma((PLANE,)),
            dma((PLANE,)),
            dma((Z - 1,)),
            dma((Z - 1,)),
            dma((NB + 2,)),
        ],
        compiler_params=pltpu.CompilerParams(
            collective_id=0, has_side_effects=True, vmem_limit_bytes=60 * 1024 * 1024
        ),
        name="sigma",
    )(pair_index, probes, phi, eigvecs, freqs, occupations, smearing, perm)


def solution(mesh):
    return jax.shard_map(
        shards,
        mesh=mesh,
        in_specs=(
            P("pair", "mode", None, None),
            P(),
            P(),
            P(),
            P(),
            P("pair", None),
            P("pair", None),
        ),
        out_specs=P("mode", None, "pair"),
        check_vma=False,
    )
```

time: 482 us -> 118 us (0.24)
  waiting for transfers between devices: 382 us -> 0 us
  Pallas kernels: 0 us -> 116 us
  local copies, waits for them, and re-layouts: 48.2 us -> 1.31 us
  between operations: 19.8 us -> 0.01 us
  matrix products: 15.9 us -> 0 us
  starting transfers between devices: 10.3 us -> 0 us
  other arithmetic: 5.15 us -> 0 us
    unnamed x4 -> x0, waiting for transfers between devices: 299 us -> none
    pallas_call x0 -> x1, Pallas kernels: none -> 116 us  [shards(): pl.pallas_call(kernel, out_shape=jax.ShapeDtypeStruct((B, 2, M // PAIRS),...]
    all_to_all x1 -> x0, waiting for transfers between devices: 82.5 us -> none  [shards(): lax.all_to_all(second, 'mode', split_axis=1, concat_axis=0, tiled=True)]
    dot_general x4 -> x0, matrix products: 15.9 us -> none  [the longest x1 5.87 us: shards(): jnp.dot(tensor.reshape(slices * modes, modes), e_one, preferred_element_t...]
    add x12 -> x0, local copies, waits for them, and re-layouts: 11.9 us -> none  [the longest x4 3.98 us: weights(): total = f_two[:, None] + f_one[None, :]]
    unnamed x16 -> x1, local copies, waits for them, and re-layouts: 12.8 us -> 1.31 us
    convert_element_type x2 -> x0, local copies, waits for them, and re-layouts: 10.2 us -> none  [the longest x1 5.73 us: shards(): first = first.astype(jnp.bfloat16).reshape(slices, modes, modes)]
    all_to_all x1 -> x0, starting transfers between devices: 10 us -> none  [shards(): lax.all_to_all(second, 'mode', split_axis=1, concat_axis=0, tiled=True)]
  transfers between devices with their start and end apart: 3 -> 0, of which waited for: 3 -> 0; matrix products, arithmetic and copies ran while one was open for 5% -> 0% of each run, Pallas kernels for 0% -> 0%
where the time goes in v1:
time: 118 us; the launch traced here: 117 us
  Pallas kernels  116 us (98%)
  local copies, waits for them, and re-layouts  1.31 us (1%)
    pallas_call x1, Pallas kernels, shards(): pl.pallas_call(kernel, out_shape=jax.ShapeDtypeStruct((B, 2, M // PAIRS),...  116 us

profile of v1, /device:TPU:8, one launch (start us, length us, event | category | flops | bytes accessed | tf_op | source)
XLA Modules:
  0.0 117.0 jit_solution(4425402672600276699)
XLA Ops:
  0.0 115.7 %sigma.1 = f32[12,2,48]{2,1,0:T(2,128)} custom-call(s32[1,3]{1,0:T(1,128)} %pidx.1, f32[1,2]{1,0:T(1,128)} %probes.1, bf16[1,12,384,384]{3,2,1,0:T(8,128)(2,1)} %phi.1, bf16[12,384,384]{2,1,0:T(8,128)(2,1)} %eig.1, f32[12,384]{1,0:T(8,128)} %freqs.1, f32[12,384]{1,0:T(8,128)} %occ.1, f32[12,384]{1,0:T(8,128)} %smear.1, bf16[384,384]{1,0:T(8,128)(2,1)} %constant.2.clone.perm), custom_call_target="tpu_custom_call" | custom-call | tf_op jit(solution)/shard_map/sigma/pallas_call | solution.py:317
  115.7 1.3 %copy.10 = f32[12,2,48]{2,1,0:T(2,128)} copy(f32[12,2,48]{2,1,0:T(2,128)} %sigma.1) | data formatting | bytes 9216

commit v2 on v1

--- a/solution.py
+++ b/solution.py
@@ -22,6 +22,8 @@
 PEERS = Z * G - 1
 PAIRS = 8
 PLANE = 15
+PIECES = ((0, 0, 12), (1, 0, 12), (2, 0, 6), (2, 6, 4), (2, 10, 2))
+NP = len(PIECES)
 
 
 def lorentz(offset, eta):
@@ -33,10 +35,10 @@
 
 
 def kernel(
-    pidx, probes, phi, eig, freqs, occ, smear, perm, out,
-    e_two_t, e_one, e_three_t, u_f, u_b, send, recv, wgt, acc, half_own, half_got, plane_src,
+    pidx, probes, phi_hbm, eig_hbm, freqs, occ, smear, perm, out,
+    phi, eig, lhs, right_s, e_two_t, e_one, e_three_t, u_f, u_b, send, recv, wgt, acc, half_own, half_got, plane_src,
     plane_got, turned, z_got,
-    a_send, a_recv, c_send, c_recv, p_send, p_recv, z_send, z_recv, local,
+    a_send, a_recv, c_send, c_recv, p_send, p_recv, z_send, z_recv, local, loads,
 ):
     mode = lax.axis_index("mode")
     pair = lax.axis_index("pair")
@@ -56,6 +58,16 @@
     def plane_back(d):
         return lax.rem(y + 4 - d // 4, 4), lax.rem(xh + (d // 2) % 2, 2), lax.rem(xl + d % 2, 2)
 
+    load_eig = pltpu.make_async_copy(eig_hbm, eig, loads.at[B // 2])
+    load_eig.start()
+
+    def load_phi(n):
+        two = pl.ds(2 * n, 2)
+        return pltpu.make_async_copy(phi_hbm.at[0, two], phi.at[two], loads.at[n])
+
+    for n in range(B // 2):
+        load_phi(n).start()
+
     barrier = pltpu.get_barrier_semaphore()
 
     def greet(i, carry):
@@ -70,6 +82,7 @@
             barrier, inc=1, device_id=(yy * 2 + hh, z * G + ll * 2 + core), device_id_type=MESH
         )
 
+    load_eig.wait()
     q_one = pidx[0, 0]
     q_two = pidx[0, 1]
     q_three = pidx[0, 2]
@@ -80,20 +93,25 @@
     e_three_t[...] = dot(perm[...], eig[q_three], ((1,), (1,))).astype(BF16)
     e_one[...] = eig[q_one]
 
-    def rotate_two(c, carry):
-        rows = dot(e_two_t[...], phi[0, c])
-        for b in range(NB):
-            u_f[b, pl.ds(c, M, stride=B), :] = rows[:, b * L : (b + 1) * L]
+    def rotate_two(n, carry):
+        load_phi(n).wait()
+        rows = dot(e_two_t[...], jnp.concatenate([phi[2 * n], phi[2 * n + 1]], axis=1))
+        for c in range(2):
+            for b in range(NB):
+                u_f[b, pl.ds(2 * n + c, M, stride=B), :] = rows[
+                    :, c * M + b * L : c * M + (b + 1) * L
+                ]
         return carry
 
-    lax.fori_loop(0, B, rotate_two, 0)
-
-    def ship(chunk, peer, zz, gg):
+    lax.fori_loop(0, B // 2, rotate_two, 0)
+
+    def ship(piece, peer, zz, gg):
+        chunk, j, nj = PIECES[piece]
         return pltpu.make_async_remote_copy(
-            src_ref=send.at[chunk, zz * G + gg],
-            dst_ref=recv.at[chunk, :, pl.ds(3 * mode, 3)],
-            send_sem=a_send.at[chunk, peer],
-            recv_sem=a_recv.at[chunk, peer],
+            src_ref=send.at[chunk, zz * G + gg, pl.ds(j, nj)],
+            dst_ref=recv.at[chunk, pl.ds(j, nj), pl.ds(3 * mode, 3)],
+            send_sem=a_send.at[piece, peer],
+            recv_sem=a_recv.at[piece, peer],
             device_id=(pair, zz * G + gg),
             device_id_type=MESH,
         )
@@ -124,15 +142,14 @@
                 :, (chunk - 1) * L : chunk * L
             ]
 
-    def ship_all(chunk, t):
+    def ship_all(piece, t):
         zz = far(t)
         for e in range(G):
-            ship(chunk, t * G + e, zz, mate(e)).start()
-
-    def ship_near(chunk):
+            ship(piece, t * G + e, zz, mate(e)).start()
+
+    def ship_near(piece):
         for e in range(1, G):
-            ship(chunk, (Z - 1) * G + e - 1, z, mate(e)).start()
-        keep(chunk).start()
+            ship(piece, (Z - 1) * G + e - 1, z, mate(e)).start()
 
     first_chunk(far(0))
     pl.semaphore_wait(barrier, PEERS + PLANE - 1)
@@ -146,6 +163,7 @@
     lax.fori_loop(1, Z - 1, step_first, 0)
     first_chunk(z)
     ship_near(0)
+    keep(0).start()
 
     def step_later(t, carry):
         later_chunks(far(t))
@@ -155,13 +173,17 @@
     lax.fori_loop(0, Z - 1, step_later, 0)
     later_chunks(z)
     ship_near(1)
-
-    def step_last(t, carry):
-        ship_all(2, t)
-        return carry
-
-    lax.fori_loop(0, Z - 1, step_last, 0)
-    ship_near(2)
+    keep(1).start()
+    keep(2).start()
+
+    for piece in range(2, NP):
+
+        def step_last(t, carry, piece=piece):
+            ship_all(piece, t)
+            return carry
+
+        lax.fori_loop(0, Z - 1, step_last, 0)
+        ship_near(piece)
 
     lane = lax.broadcasted_iota(jnp.int32, (B, M), 1)
     mine = lane == mode * B + lax.broadcasted_iota(jnp.int32, (B, M), 0)
@@ -190,44 +212,69 @@
     acc[...] = jnp.zeros_like(acc)
     span = M // G
 
-    def take(chunk):
+    def rotated(chunk, jp):
+        block = jnp.concatenate(
+            [recv.at[chunk, 2 * jp + s].reshape(M, L)[...] for s in range(2)], axis=1
+        )
+        rot = dot(e_three_t[...], block).astype(BF16)
+        wide = rot.astype(F32)
+        weighted = []
+        for w in range(2):
+            row = jnp.concatenate(
+                [wgt[w, 2 * jp + s, :, chunk * L : (chunk + 1) * L] for s in range(2)], axis=1
+            )
+            weighted.append((wide * row).astype(BF16))
+        return rot, weighted
+
+    hole = jnp.zeros((L - span, 2 * L), BF16)
+
+    def arrive(piece):
         def wait_one(i, carry):
-            ship(chunk, i, z, mate(1)).wait_recv()
+            ship(piece, i, z, mate(1)).wait_recv()
             return carry
 
         lax.fori_loop(0, PEERS, wait_one, 0)
-        keep(chunk).wait()
-
-        def gram(jp, carry):
-            block = jnp.concatenate(
-                [recv.at[chunk, 2 * jp + s].reshape(M, L)[...] for s in range(2)], axis=1
-            )
-            rot = dot(e_three_t[...], block).astype(BF16)
-            hole = jnp.zeros((L - span, 2 * L), BF16)
-            parts = []
+
+    def gram(chunk, jp):
+        rot, weighted = rotated(chunk, jp)
+        parts = []
+        for k in range(G):
+            parts += [rot[k * span : (k + 1) * span], hole]
+        right = jnp.concatenate(parts, axis=0)
+        for w in range(2):
+            part = dot(weighted[w], right, ((1,), (1,)))
             for k in range(G):
-                parts += [rot[k * span : (k + 1) * span], hole]
-            right = jnp.concatenate(parts, axis=0)
-            wide = rot.astype(F32)
-            for w in range(2):
-                row = jnp.concatenate(
-                    [wgt[w, 2 * jp + s, :, chunk * L : (chunk + 1) * L] for s in range(2)],
-                    axis=1,
-                )
-                part = dot((wide * row).astype(BF16), right, ((1,), (1,)))
-                for k in range(G):
-                    acc[k, w * M : (w + 1) * M, :] += part[:, k * L : (k + 1) * L]
+                acc[k, w * M : (w + 1) * M, :] += part[:, k * L : (k + 1) * L]
+
+    for piece in range(NP):
+        chunk, j, nj = PIECES[piece]
+        arrive(piece)
+        if j == 0:
+            keep(chunk).wait()
+
+        def step_gram(jp, carry, chunk=chunk):
+            gram(chunk, jp)
             return carry
 
-        lax.fori_loop(0, B // 2, gram, 0)
-
-    for chunk in range(NB):
-        take(chunk)
-
-    for s in range(2):
-        half_own.at[s].reshape(2 * M, L)[...] = acc[2 * s + 1 - core].astype(BF16)
+        last = piece == NP - 1
+        lax.fori_loop(j // 2, (j + nj) // 2 - last, step_gram, 0)
+
+    rot, weighted = rotated(NB - 1, B // 2 - 1)
+    for k in range(G):
+        right_s[k] = jnp.concatenate([rot[k * span : (k + 1) * span], hole], axis=0)
+    for w in range(2):
+        lhs[w * M : (w + 1) * M] = weighted[w]
+
+    def last_lanes(c):
+        right = jnp.concatenate([right_s[2 * s + c] for s in range(2)], axis=0)
+        return dot(lhs[...], right, ((1,), (1,)))
+
+    part = last_lanes(1 - core)
     swaps = []
     for s in range(2):
+        half_own.at[s].reshape(2 * M, L)[...] = (
+            acc[2 * s + 1 - core] + part[:, s * L : (s + 1) * L]
+        ).astype(BF16)
         swap = pltpu.make_async_remote_copy(
             src_ref=half_own.at[s],
             dst_ref=half_got.at[s],
@@ -238,6 +285,9 @@
         )
         swap.start()
         swaps.append(swap)
+    part = last_lanes(core)
+    for s in range(2):
+        acc[2 * s + core] += part[:, s * L : (s + 1) * L]
     for s in range(2):
         swaps[s].wait_recv()
         both = acc[2 * s + core] + half_got.at[s].reshape(2 * M, L)[...].astype(F32)
@@ -260,10 +310,9 @@
     kept = pltpu.make_async_copy(plane_src.at[xl, :, :, pair], plane_got.at[0], local.at[NB])
     kept.start()
     kept.wait()
-    for hop in hops:
-        hop.wait_recv()
     whole = plane_got.at[0].reshape(wide_rows, L)[...].astype(F32)
     for d in range(1, PLANE + 1):
+        hops[d - 1].wait_recv()
         whole = whole + plane_got.at[d].reshape(wide_rows, L)[...].astype(F32)
 
     square = jnp.concatenate([whole, jnp.zeros((L - wide_rows, L), F32)], axis=0)
@@ -284,10 +333,9 @@
     stay = pltpu.make_async_copy(turned.at[pl.ds(3 * z, 3)], z_got.at[0], local.at[NB + 1])
     stay.start()
     stay.wait()
-    for rise in rises:
-        rise.wait_recv()
     result = z_got.at[0].reshape(B, L)[...]
     for d in range(1, Z):
+        rises[d - 1].wait_recv()
         result = result + z_got.at[d].reshape(B, L)[...]
 
     cols = M // PAIRS
@@ -298,8 +346,8 @@
         out[:, w, :] = jnp.where(row_id == col_id, 0.0, result[:, w * cols : (w + 1) * cols] * scale)
 
     def sent(i, carry):
-        for chunk in range(NB):
-            ship(chunk, i, z, mate(1)).wait_send()
+        for piece in range(NP):
+            ship(piece, i, z, mate(1)).wait_send()
         return carry
 
     lax.fori_loop(0, PEERS, sent, 0)
@@ -312,14 +360,19 @@
     natural = (k % (M // G)) // B * (G * B) + k // (M // G) * B + k % B
     perm = jnp.asarray(np.equal(natural[:, None], k[None, :]), BF16)
     vmem = pl.BlockSpec(memory_space=pltpu.VMEM)
+    hbm = pl.BlockSpec(memory_space=pl.ANY)
     smem = pl.BlockSpec(memory_space=pltpu.SMEM)
     dma = pltpu.SemaphoreType.DMA
     return pl.pallas_call(
         kernel,
         out_shape=jax.ShapeDtypeStruct((B, 2, M // PAIRS), F32),
-        in_specs=[smem, smem] + [vmem] * 6,
+        in_specs=[smem, smem, hbm, hbm] + [vmem] * 4,
         out_specs=vmem,
         scratch_shapes=[
+            pltpu.VMEM((B, M, M), BF16),
+            pltpu.VMEM(eigvecs.shape, BF16),
+            pltpu.VMEM((2 * M, 2 * L), BF16),
+            pltpu.VMEM((G, L, 2 * L), BF16),
             pltpu.VMEM((M, M), BF16),
             pltpu.VMEM((M, M), BF16),
             pltpu.VMEM((M, M), BF16),
@@ -335,8 +388,8 @@
             pltpu.VMEM((PLANE + 1, 2, G, 3, 4, L), BF16),
             pltpu.VMEM((L // 4, 4, L), F32),
             pltpu.VMEM((Z, 3, 4, L), F32),
-            dma((NB, PEERS)),
-            dma((NB, PEERS)),
+            dma((NP, PEERS)),
+            dma((NP, PEERS)),
             dma((2,)),
             dma((2,)),
             dma((PLANE,)),
@@ -344,6 +397,7 @@
             dma((Z - 1,)),
             dma((Z - 1,)),
             dma((NB + 2,)),
+            dma((B // 2 + 1,)),
         ],
         compiler_params=pltpu.CompilerParams(
             collective_id=0, has_side_effects=True, vmem_limit_bytes=60 * 1024 * 1024

time: 118 us -> 112 us (0.949)
  Pallas kernels: 116 us -> 110 us
    pallas_call x1, Pallas kernels: 116 us -> 110 us  [shards(): pl.pallas_call(kernel, out_shape=jax.ShapeDtypeStruct((B, 2, M // PAIRS),...]
where the time goes in v2:
time: 112 us
  Pallas kernels  110 us (98%)
  local copies, waits for them, and re-layouts  1.31 us (1%)
    pallas_call x1, Pallas kernels, shards(): pl.pallas_call(kernel, out_shape=jax.ShapeDtypeStruct((B, 2, M // PAIRS),...  110 us

profile of v2, /device:TPU:8, one launch (start us, length us, event | category | flops | bytes accessed | tf_op | source)
XLA Modules:
  0.0 111.7 jit_solution(9677902167869971144)
XLA Ops:
  0.0 110.4 %sigma.1 = f32[12,2,48]{2,1,0:T(2,128)} custom-call(s32[1,3]{1,0:T(1,128)} %pidx.1, f32[1,2]{1,0:T(1,128)} %probes.1, bf16[1,12,384,384]{3,2,1,0:T(8,128)(2,1)} %phi_hbm.1, bf16[12,384,384]{2,1,0:T(8,128)(2,1)} %eig_hbm.1, f32[12,384]{1,0:T(8,128)} %freqs.1, f32[12,384]{1,0:T(8,128)} %occ.1, f32[12,384]{1,0:T(8,128)} %smear.1, ...), custom_call_target="tpu_custom_call" | custom-call | tf_op jit(solution)/shard_map/sigma/pallas_call | solution.py:366
  110.4 1.3 %copy.10 = f32[12,2,48]{2,1,0:T(2,128)} copy(f32[12,2,48]{2,1,0:T(2,128)} %sigma.1) | data formatting | bytes 9216

commit v3 on v2

--- a/solution.py
+++ b/solution.py
@@ -2,7 +2,6 @@
 
 import jax
 import jax.numpy as jnp
-import numpy as np
 from jax import lax
 from jax.experimental import pallas as pl
 from jax.experimental.pallas import tpu as pltpu
@@ -35,8 +34,8 @@
 
 
 def kernel(
-    pidx, probes, phi_hbm, eig_hbm, freqs, occ, smear, perm, out,
-    phi, eig, lhs, right_s, e_two_t, e_one, e_three_t, u_f, u_b, send, recv, wgt, acc, half_own, half_got, plane_src,
+    pidx, probes, phi_hbm, eig_hbm, freqs_hbm, occ_hbm, smear_hbm, out,
+    phi, eig, freqs, occ, smear, u_part, send_first, lhs, right_s, e_two_t, e_one, e_three_t, u_f, send, recv, wgt, acc, half_own, half_got, plane_src,
     plane_got, turned, z_got,
     a_send, a_recv, c_send, c_recv, p_send, p_recv, z_send, z_recv, local, loads,
 ):
@@ -67,6 +66,14 @@
 
     for n in range(B // 2):
         load_phi(n).start()
+    tables = [
+        pltpu.make_async_copy(source, table, loads.at[B // 2 + 1 + n])
+        for n, (source, table) in enumerate(
+            ((freqs_hbm, freqs), (occ_hbm, occ), (smear_hbm, smear))
+        )
+    ]
+    for table in tables:
+        table.start()
 
     barrier = pltpu.get_barrier_semaphore()
 
@@ -90,80 +97,110 @@
     cols_i = lax.broadcasted_iota(jnp.int32, (M, M), 1)
     eye = (rows_i == cols_i).astype(F32).astype(BF16)
     e_two_t[...] = dot(eye, eig[q_two], ((1,), (1,))).astype(BF16)
-    e_three_t[...] = dot(perm[...], eig[q_three], ((1,), (1,))).astype(BF16)
     e_one[...] = eig[q_one]
 
     def rotate_two(n, carry):
         load_phi(n).wait()
         rows = dot(e_two_t[...], jnp.concatenate([phi[2 * n], phi[2 * n + 1]], axis=1))
         for c in range(2):
+            at = 2 * lax.rem(n, 2) + c
             for b in range(NB):
-                u_f[b, pl.ds(2 * n + c, M, stride=B), :] = rows[
-                    :, c * M + b * L : c * M + (b + 1) * L
-                ]
+                value = rows[:, c * M + b * L : c * M + (b + 1) * L]
+                u_f[b, pl.ds(2 * n + c, M, stride=B), :] = value
+                u_part[b, pl.ds(at, M, stride=4), :] = value
         return carry
 
-    lax.fori_loop(0, B // 2, rotate_two, 0)
-
-    def ship(piece, peer, zz, gg):
+    def ship_first(group, zz, gg):
+        return pltpu.make_async_remote_copy(
+            src_ref=send_first.at[group, zz * G + gg],
+            dst_ref=recv.at[0, :, 3 * mode + group],
+            send_sem=a_send.at[0],
+            recv_sem=a_recv.at[0],
+            device_id=(pair, zz * G + gg),
+            device_id_type=MESH,
+        )
+
+    def keep_first(group):
+        return pltpu.make_async_copy(
+            send_first.at[group, mode], recv.at[0, :, 3 * mode + group], local.at[group]
+        )
+
+    def ship(piece, zz, gg):
         chunk, j, nj = PIECES[piece]
         return pltpu.make_async_remote_copy(
-            src_ref=send.at[chunk, zz * G + gg, pl.ds(j, nj)],
+            src_ref=send.at[chunk - 1, zz * G + gg, pl.ds(j, nj)],
             dst_ref=recv.at[chunk, pl.ds(j, nj), pl.ds(3 * mode, 3)],
-            send_sem=a_send.at[piece, peer],
-            recv_sem=a_recv.at[piece, peer],
+            send_sem=a_send.at[piece],
+            recv_sem=a_recv.at[piece],
             device_id=(pair, zz * G + gg),
             device_id_type=MESH,
         )
 
     def keep(chunk):
         return pltpu.make_async_copy(
-            send.at[chunk, mode], recv.at[chunk, :, pl.ds(3 * mode, 3)], local.at[chunk]
+            send.at[chunk - 1, mode], recv.at[chunk, :, pl.ds(3 * mode, 3)], local.at[chunk + 2]
+        )
+
+    def everyone(piece):
+        chunk, j, nj = PIECES[piece]
+        block = recv.at[chunk, pl.ds(j, nj), pl.ds(0, 3 * PEERS)]
+        return pltpu.make_async_remote_copy(
+            src_ref=block,
+            dst_ref=block,
+            send_sem=a_send.at[piece],
+            recv_sem=a_recv.at[piece],
+            device_id=(pair, z * G + mate(1)),
+            device_id_type=MESH,
         )
 
     def far(t):
         h = (t + 1) // 2
         return lax.rem(z + 4 + (1 - 2 * lax.rem(t, 2)) * h, Z)
 
-    def first_chunk(zz):
+    def first_group(group, zz):
+        size = M * 4 // Z
+        start = pl.multiple_of(zz * size, size)
+        rows = jnp.concatenate([u_part[b, pl.ds(start, size), :] for b in range(NB)], axis=1)
+        done = dot(rows.astype(BF16), e_one[:, :L]).astype(BF16)
+        send_first.at[group, pl.ds(zz * G, G)].reshape(size, L)[...] = done
+
+    def later_chunks(zz):
         start = pl.multiple_of(zz * (G * ROWS), G * ROWS)
         rows = jnp.concatenate(
             [u_f[b, pl.ds(start, G * ROWS), :] for b in range(NB)], axis=1
         ).astype(BF16)
-        u_b[pl.ds(start, G * ROWS), :] = rows
-        done = dot(rows, e_one[:, :L]).astype(BF16)
-        send.at[0, pl.ds(zz * G, G)].reshape(G * ROWS, L)[...] = done
-
-    def later_chunks(zz):
-        start = pl.multiple_of(zz * (G * ROWS), G * ROWS)
-        done = dot(u_b[pl.ds(start, G * ROWS), :], e_one[:, L:]).astype(BF16)
+        done = dot(rows, e_one[:, L:]).astype(BF16)
         for chunk in range(1, NB):
-            send.at[chunk, pl.ds(zz * G, G)].reshape(G * ROWS, L)[...] = done[
+            send.at[chunk - 1, pl.ds(zz * G, G)].reshape(G * ROWS, L)[...] = done[
                 :, (chunk - 1) * L : chunk * L
             ]
 
     def ship_all(piece, t):
         zz = far(t)
         for e in range(G):
-            ship(piece, t * G + e, zz, mate(e)).start()
+            ship(piece, zz, mate(e)).start()
 
     def ship_near(piece):
         for e in range(1, G):
-            ship(piece, (Z - 1) * G + e - 1, z, mate(e)).start()
-
-    first_chunk(far(0))
-    pl.semaphore_wait(barrier, PEERS + PLANE - 1)
-    ship_all(0, 0)
-
-    def step_first(t, carry):
-        first_chunk(far(t))
-        ship_all(0, t)
-        return carry
-
-    lax.fori_loop(1, Z - 1, step_first, 0)
-    first_chunk(z)
-    ship_near(0)
-    keep(0).start()
+            ship(piece, z, mate(e)).start()
+
+    for group in range(3):
+        lax.fori_loop(2 * group, 2 * group + 2, rotate_two, 0)
+        if group == 0:
+            pl.semaphore_wait(barrier, PEERS + PLANE - 1)
+
+        def step_first(t, carry, group=group):
+            zz = far(t)
+            first_group(group, zz)
+            for e in range(G):
+                ship_first(group, zz, mate(e)).start()
+            return carry
+
+        lax.fori_loop(0, Z - 1, step_first, 0)
+        first_group(group, z)
+        for e in range(1, G):
+            ship_first(group, z, mate(e)).start()
+        keep_first(group).start()
 
     def step_later(t, carry):
         later_chunks(far(t))
@@ -173,8 +210,8 @@
     lax.fori_loop(0, Z - 1, step_later, 0)
     later_chunks(z)
     ship_near(1)
-    keep(1).start()
-    keep(2).start()
+    for chunk in range(1, NB):
+        keep(chunk).start()
 
     for piece in range(2, NP):
 
@@ -185,6 +222,16 @@
         lax.fori_loop(0, Z - 1, step_last, 0)
         ship_near(piece)
 
+    row = lax.broadcasted_iota(jnp.int32, (M, 1), 0)
+    block = sum((row >= n * (M // G)).astype(jnp.int32) for n in range(1, G))
+    within = row - block * (M // G)
+    chip = sum((within >= n * B).astype(jnp.int32) for n in range(1, Z))
+    natural = within + (G - 1) * B * chip + B * block
+    perm = (natural == cols_i).astype(F32).astype(BF16)
+    e_three_t[...] = dot(perm, eig[q_three], ((1,), (1,))).astype(BF16)
+
+    for table in tables:
+        table.wait()
     lane = lax.broadcasted_iota(jnp.int32, (B, M), 1)
     mine = lane == mode * B + lax.broadcasted_iota(jnp.int32, (B, M), 0)
 
@@ -228,13 +275,6 @@
 
     hole = jnp.zeros((L - span, 2 * L), BF16)
 
-    def arrive(piece):
-        def wait_one(i, carry):
-            ship(piece, i, z, mate(1)).wait_recv()
-            return carry
-
-        lax.fori_loop(0, PEERS, wait_one, 0)
-
     def gram(chunk, jp):
         rot, weighted = rotated(chunk, jp)
         parts = []
@@ -248,8 +288,11 @@
 
     for piece in range(NP):
         chunk, j, nj = PIECES[piece]
-        arrive(piece)
-        if j == 0:
+        everyone(piece).wait_recv()
+        if chunk == 0:
+            for group in range(3):
+                keep_first(group).wait()
+        elif j == 0:
             keep(chunk).wait()
 
         def step_gram(jp, carry, chunk=chunk):
@@ -293,49 +336,63 @@
         both = acc[2 * s + core] + half_got.at[s].reshape(2 * M, L)[...].astype(F32)
         plane_src.at[s].reshape(2 * M, L)[...] = both.astype(BF16)
 
-    hops = []
     for d in range(1, PLANE + 1):
         yy, hh, ll = plane_peer(d)
         hop = pltpu.make_async_remote_copy(
             src_ref=plane_src.at[ll, :, :, yy * 2 + hh],
             dst_ref=plane_got.at[d],
-            send_sem=p_send.at[d - 1],
-            recv_sem=p_recv.at[d - 1],
+            send_sem=p_send,
+            recv_sem=p_recv,
             device_id=(yy * 2 + hh, z * G + ll * 2 + core),
             device_id_type=MESH,
         )
         hop.start()
-        hops.append(hop)
     wide_rows = 2 * M // PAIRS
-    kept = pltpu.make_async_copy(plane_src.at[xl, :, :, pair], plane_got.at[0], local.at[NB])
+    kept = pltpu.make_async_copy(plane_src.at[xl, :, :, pair], plane_got.at[0], local.at[6])
     kept.start()
     kept.wait()
+    others = plane_got.at[pl.ds(1, PLANE)]
+    hops = pltpu.make_async_remote_copy(
+        src_ref=others,
+        dst_ref=others,
+        send_sem=p_send,
+        recv_sem=p_recv,
+        device_id=(pair, z * G + mate(2)),
+        device_id_type=MESH,
+    )
+    hops.wait_recv()
     whole = plane_got.at[0].reshape(wide_rows, L)[...].astype(F32)
     for d in range(1, PLANE + 1):
-        hops[d - 1].wait_recv()
         whole = whole + plane_got.at[d].reshape(wide_rows, L)[...].astype(F32)
 
     square = jnp.concatenate([whole, jnp.zeros((L - wide_rows, L), F32)], axis=0)
     turned.reshape(L, L)[...] = square.T
-    rises = []
     for d in range(1, Z):
         zz = lax.rem(z + d, Z)
         rise = pltpu.make_async_remote_copy(
             src_ref=turned.at[pl.ds(3 * zz, 3)],
             dst_ref=z_got.at[d],
-            send_sem=z_send.at[d - 1],
-            recv_sem=z_recv.at[d - 1],
+            send_sem=z_send,
+            recv_sem=z_recv,
             device_id=(pair, zz * G + g),
             device_id_type=MESH,
         )
         rise.start()
-        rises.append(rise)
-    stay = pltpu.make_async_copy(turned.at[pl.ds(3 * z, 3)], z_got.at[0], local.at[NB + 1])
+    stay = pltpu.make_async_copy(turned.at[pl.ds(3 * z, 3)], z_got.at[0], local.at[7])
     stay.start()
     stay.wait()
+    others = z_got.at[pl.ds(1, Z - 1)]
+    rises = pltpu.make_async_remote_copy(
+        src_ref=others,
+        dst_ref=others,
+        send_sem=z_send,
+        recv_sem=z_recv,
+        device_id=(pair, z * G + mate(1)),
+        device_id_type=MESH,
+    )
+    rises.wait_recv()
     result = z_got.at[0].reshape(B, L)[...]
     for d in range(1, Z):
-        rises[d - 1].wait_recv()
         result = result + z_got.at[d].reshape(B, L)[...]
 
     cols = M // PAIRS
@@ -345,20 +402,13 @@
     for w in range(2):
         out[:, w, :] = jnp.where(row_id == col_id, 0.0, result[:, w * cols : (w + 1) * cols] * scale)
 
-    def sent(i, carry):
-        for piece in range(NP):
-            ship(piece, i, z, mate(1)).wait_send()
-        return carry
-
-    lax.fori_loop(0, PEERS, sent, 0)
-    for copy in swaps + hops + rises:
+    for piece in range(NP):
+        everyone(piece).wait_send()
+    for copy in swaps + [hops, rises]:
         copy.wait_send()
 
 
 def shards(phi, eigvecs, freqs, occupations, smearing, probes, pair_index):
-    k = np.arange(M)
-    natural = (k % (M // G)) // B * (G * B) + k // (M // G) * B + k % B
-    perm = jnp.asarray(np.equal(natural[:, None], k[None, :]), BF16)
     vmem = pl.BlockSpec(memory_space=pltpu.VMEM)
     hbm = pl.BlockSpec(memory_space=pl.ANY)
     smem = pl.BlockSpec(memory_space=pltpu.SMEM)
@@ -366,19 +416,23 @@
     return pl.pallas_call(
         kernel,
         out_shape=jax.ShapeDtypeStruct((B, 2, M // PAIRS), F32),
-        in_specs=[smem, smem, hbm, hbm] + [vmem] * 4,
+        in_specs=[smem, smem] + [hbm] * 5,
         out_specs=vmem,
         scratch_shapes=[
             pltpu.VMEM((B, M, M), BF16),
             pltpu.VMEM(eigvecs.shape, BF16),
+            pltpu.VMEM(freqs.shape, F32),
+            pltpu.VMEM(freqs.shape, F32),
+            pltpu.VMEM(freqs.shape, F32),
+            pltpu.VMEM((NB, M * 4, L), F32),
+            pltpu.VMEM((3, Z * G, B, 4, L), BF16),
             pltpu.VMEM((2 * M, 2 * L), BF16),
             pltpu.VMEM((G, L, 2 * L), BF16),
             pltpu.VMEM((M, M), BF16),
             pltpu.VMEM((M, M), BF16),
             pltpu.VMEM((M, M), BF16),
             pltpu.VMEM((NB, M * B, L), F32),
-            pltpu.VMEM((M * B, M), BF16),
-            pltpu.VMEM((NB, Z * G, B, 3, 4, L), BF16),
+            pltpu.VMEM((NB - 1, Z * G, B, 3, 4, L), BF16),
             pltpu.VMEM((NB, B, M // 4, 4, L), BF16),
             pltpu.VMEM((2, B, 1, M), F32),
             pltpu.VMEM((G, 2 * M, L), F32),
@@ -388,22 +442,22 @@
             pltpu.VMEM((PLANE + 1, 2, G, 3, 4, L), BF16),
             pltpu.VMEM((L // 4, 4, L), F32),
             pltpu.VMEM((Z, 3, 4, L), F32),
-            dma((NP, PEERS)),
-            dma((NP, PEERS)),
+            dma((NP,)),
+            dma((NP,)),
             dma((2,)),
             dma((2,)),
-            dma((PLANE,)),
-            dma((PLANE,)),
-            dma((Z - 1,)),
-            dma((Z - 1,)),
-            dma((NB + 2,)),
-            dma((B // 2 + 1,)),
+            dma,
+            dma,
+            dma,
+            dma,
+            dma((8,)),
+            dma((B // 2 + 4,)),
         ],
         compiler_params=pltpu.CompilerParams(
             collective_id=0, has_side_effects=True, vmem_limit_bytes=60 * 1024 * 1024
         ),
         name="sigma",
-    )(pair_index, probes, phi, eigvecs, freqs, occupations, smearing, perm)
+    )(pair_index, probes, phi, eigvecs, freqs, occupations, smearing)
 
 
 def solution(mesh):

time: 112 us -> 107 us (0.955)
  Pallas kernels: 110 us -> 106 us
    pallas_call x1, Pallas kernels: 110 us -> 106 us  [shards(): pl.pallas_call(kernel, out_shape=jax.ShapeDtypeStruct((B, 2, M // PAIRS),...]
where the time goes in v3:
time: 107 us
  Pallas kernels  106 us (99%)
  local copies, waits for them, and re-layouts  1.31 us (1%)
    pallas_call x1, Pallas kernels, shards(): pl.pallas_call(kernel, out_shape=jax.ShapeDtypeStruct((B, 2, M // PAIRS),...  106 us

profile of v3, /device:TPU:8, one launch (start us, length us, event | category | flops | bytes accessed | tf_op | source)
XLA Modules:
  0.0 106.9 jit_solution(6359037307319726237)
XLA Ops:
  0.0 105.6 %sigma.1 = f32[12,2,48]{2,1,0:T(2,128)} custom-call(s32[1,3]{1,0:T(1,128)} %pidx.1, f32[1,2]{1,0:T(1,128)} %probes.1, bf16[1,12,384,384]{3,2,1,0:T(8,128)(2,1)} %phi_hbm.1, bf16[12,384,384]{2,1,0:T(8,128)(2,1)} %eig_hbm.1, f32[12,384]{1,0:T(8,128)} %freqs_hbm.1, f32[12,384]{1,0:T(8,128)} %occ_hbm.1, f32[12,384]{1,0:T(8,128)} %smear_hbm.1), custom_call_target="tpu_custom_call" | custom-call | tf_op jit(solution)/shard_map/sigma/pallas_call | solution.py:416
  105.6 1.3 %copy.9 = f32[12,2,48]{2,1,0:T(2,128)} copy(f32[12,2,48]{2,1,0:T(2,128)} %sigma.1) | data formatting | bytes 9216

commit v4 on v3

--- a/solution.py
+++ b/solution.py
@@ -23,6 +23,7 @@
 PLANE = 15
 PIECES = ((0, 0, 12), (1, 0, 12), (2, 0, 6), (2, 6, 4), (2, 10, 2))
 NP = len(PIECES)
+HOPS = (10, 9, 11, 6, 14, 8, 5, 7, 13, 15, 2, 4, 12, 1, 3)
 
 
 def lorentz(offset, eta):
@@ -34,9 +35,9 @@
 
 
 def kernel(
-    pidx, probes, phi_hbm, eig_hbm, freqs_hbm, occ_hbm, smear_hbm, out,
-    phi, eig, freqs, occ, smear, u_part, send_first, lhs, right_s, e_two_t, e_one, e_three_t, u_f, send, recv, wgt, acc, half_own, half_got, plane_src,
-    plane_got, turned, z_got,
+    pidx_hbm, probes_hbm, phi_hbm, eig_hbm, freqs_hbm, occ_hbm, smear_hbm, out,
+    pidx, probes, phi, eig, freqs, occ, smear, u_part, send_first, lhs, right_s, e_two_t, e_one, e_three_t, u_f, send, recv, wgt, acc, half_own, half_got, plane_src,
+    plane_got, merged, turned, z_got,
     a_send, a_recv, c_send, c_recv, p_send, p_recv, z_send, z_recv, local, loads,
 ):
     mode = lax.axis_index("mode")
@@ -57,8 +58,36 @@
     def plane_back(d):
         return lax.rem(y + 4 - d // 4, 4), lax.rem(xh + (d // 2) % 2, 2), lax.rem(xl + d % 2, 2)
 
+    def far(t):
+        h = (t + 1) // 2
+        return lax.rem(z + 4 + (1 - 2 * lax.rem(t, 2)) * h, Z)
+
+    load_index = pltpu.make_async_copy(pidx_hbm, pidx, loads.at[B // 2 + 5])
+    load_index.start()
     load_eig = pltpu.make_async_copy(eig_hbm, eig, loads.at[B // 2])
     load_eig.start()
+
+    barrier = pltpu.get_barrier_semaphore()
+
+    def greet(t, carry):
+        for gg in range(G):
+            pl.semaphore_signal(
+                barrier, inc=1, device_id=(pair, far(t) * G + gg), device_id_type=MESH
+            )
+        return carry
+
+    lax.fori_loop(0, 3, greet, 0)
+    for d in HOPS:
+        if d >= 2:
+            yy, hh, ll = plane_back(d)
+            pl.semaphore_signal(
+                barrier, inc=1, device_id=(yy * 2 + hh, z * G + ll * 2 + core), device_id_type=MESH
+            )
+    lax.fori_loop(3, Z - 1, greet, 0)
+    for e in range(1, G):
+        pl.semaphore_signal(
+            barrier, inc=1, device_id=(pair, z * G + mate(e)), device_id_type=MESH
+        )
 
     def load_phi(n):
         two = pl.ds(2 * n, 2)
@@ -69,26 +98,13 @@
     tables = [
         pltpu.make_async_copy(source, table, loads.at[B // 2 + 1 + n])
         for n, (source, table) in enumerate(
-            ((freqs_hbm, freqs), (occ_hbm, occ), (smear_hbm, smear))
+            ((freqs_hbm, freqs), (occ_hbm, occ), (smear_hbm, smear), (probes_hbm, probes))
         )
     ]
     for table in tables:
         table.start()
 
-    barrier = pltpu.get_barrier_semaphore()
-
-    def greet(i, carry):
-        other = lax.rem(mode + 1 + i, Z * G)
-        pl.semaphore_signal(barrier, inc=1, device_id=(pair, other), device_id_type=MESH)
-        return carry
-
-    lax.fori_loop(0, PEERS, greet, 0)
-    for d in range(2, PLANE + 1):
-        yy, hh, ll = plane_back(d)
-        pl.semaphore_signal(
-            barrier, inc=1, device_id=(yy * 2 + hh, z * G + ll * 2 + core), device_id_type=MESH
-        )
-
+    load_index.wait()
     load_eig.wait()
     q_one = pidx[0, 0]
     q_two = pidx[0, 1]
@@ -152,10 +168,6 @@
             device_id=(pair, z * G + mate(1)),
             device_id_type=MESH,
         )
-
-    def far(t):
-        h = (t + 1) // 2
-        return lax.rem(z + 4 + (1 - 2 * lax.rem(t, 2)) * h, Z)
 
     def first_group(group, zz):
         size = M * 4 // Z
@@ -306,51 +318,63 @@
     for k in range(G):
         right_s[k] = jnp.concatenate([rot[k * span : (k + 1) * span], hole], axis=0)
     for w in range(2):
-        lhs[w * M : (w + 1) * M] = weighted[w]
-
-    def last_lanes(c):
+        lhs[w] = weighted[w]
+
+    def last_lanes(c, w):
         right = jnp.concatenate([right_s[2 * s + c] for s in range(2)], axis=0)
-        return dot(lhs[...], right, ((1,), (1,)))
-
-    part = last_lanes(1 - core)
+        return dot(lhs[w], right, ((1,), (1,)))
+
     swaps = []
-    for s in range(2):
-        half_own.at[s].reshape(2 * M, L)[...] = (
-            acc[2 * s + 1 - core] + part[:, s * L : (s + 1) * L]
-        ).astype(BF16)
+    for w in range(2):
+        part = last_lanes(1 - core, w)
+        for s in range(2):
+            half_own.at[w, s].reshape(M, L)[...] = (
+                acc[2 * s + 1 - core, w * M : (w + 1) * M] + part[:, s * L : (s + 1) * L]
+            ).astype(BF16)
         swap = pltpu.make_async_remote_copy(
-            src_ref=half_own.at[s],
-            dst_ref=half_got.at[s],
-            send_sem=c_send.at[s],
-            recv_sem=c_recv.at[s],
+            src_ref=half_own.at[w],
+            dst_ref=half_got.at[w],
+            send_sem=c_send.at[w],
+            recv_sem=c_recv.at[w],
             device_id=(pair, z * G + xl * 2 + 1 - core),
             device_id_type=MESH,
         )
         swap.start()
         swaps.append(swap)
-    part = last_lanes(core)
-    for s in range(2):
-        acc[2 * s + core] += part[:, s * L : (s + 1) * L]
-    for s in range(2):
-        swaps[s].wait_recv()
-        both = acc[2 * s + core] + half_got.at[s].reshape(2 * M, L)[...].astype(F32)
-        plane_src.at[s].reshape(2 * M, L)[...] = both.astype(BF16)
-
-    for d in range(1, PLANE + 1):
-        yy, hh, ll = plane_peer(d)
-        hop = pltpu.make_async_remote_copy(
-            src_ref=plane_src.at[ll, :, :, yy * 2 + hh],
-            dst_ref=plane_got.at[d],
-            send_sem=p_send,
-            recv_sem=p_recv,
-            device_id=(yy * 2 + hh, z * G + ll * 2 + core),
-            device_id_type=MESH,
-        )
-        hop.start()
-    wide_rows = 2 * M // PAIRS
-    kept = pltpu.make_async_copy(plane_src.at[xl, :, :, pair], plane_got.at[0], local.at[6])
-    kept.start()
-    kept.wait()
+    for w in range(2):
+        part = last_lanes(core, w)
+        for s in range(2):
+            acc[2 * s + core, w * M : (w + 1) * M] += part[:, s * L : (s + 1) * L]
+
+    spare = lax.broadcasted_iota(jnp.int32, (span, L), 1) >= span
+    rest = L - span
+    kept = []
+    for w in range(2):
+        swaps[w].wait_recv()
+        for s in range(2):
+            got = half_got.at[w, s].reshape(M, L)[...].astype(F32)
+            both = acc[2 * s + core, w * M : (w + 1) * M] + got
+            for n in range(G - 1):
+                moved = pltpu.roll(both[(G - 1) * span :], span - rest * n, 1)
+                packed = jnp.where(spare, moved, both[n * span : (n + 1) * span])
+                plane_src.at[w, s, n].reshape(span, L)[...] = packed.astype(BF16)
+        for d in HOPS:
+            yy, hh, ll = plane_peer(d)
+            pltpu.make_async_remote_copy(
+                src_ref=plane_src.at[w, ll, :, yy * 2 + hh],
+                dst_ref=plane_got.at[d, w],
+                send_sem=p_send,
+                recv_sem=p_recv,
+                device_id=(yy * 2 + hh, z * G + ll * 2 + core),
+                device_id_type=MESH,
+            ).start()
+        kept.append(
+            pltpu.make_async_copy(plane_src.at[w, xl, :, pair], plane_got.at[0, w], local.at[6 + w])
+        )
+        kept[w].start()
+    for w in range(2):
+        kept[w].wait()
+        merged[w, G - 1] = jnp.zeros((3, 4, L), F32)
     others = plane_got.at[pl.ds(1, PLANE)]
     hops = pltpu.make_async_remote_copy(
         src_ref=others,
@@ -361,24 +385,34 @@
         device_id_type=MESH,
     )
     hops.wait_recv()
-    whole = plane_got.at[0].reshape(wide_rows, L)[...].astype(F32)
-    for d in range(1, PLANE + 1):
-        whole = whole + plane_got.at[d].reshape(wide_rows, L)[...].astype(F32)
-
-    square = jnp.concatenate([whole, jnp.zeros((L - wide_rows, L), F32)], axis=0)
-    turned.reshape(L, L)[...] = square.T
-    for d in range(1, Z):
+    some = (G - 1) * B
+    for w in range(2):
+        whole = plane_got.at[0, w].reshape(some, L)[...].astype(F32)
+        for d in range(1, PLANE + 1):
+            whole = whole + plane_got.at[d, w].reshape(some, L)[...].astype(F32)
+        merged.at[w, pl.ds(0, G - 1)].reshape(some, L)[...] = whole
+
+    wide_rows = 2 * M // PAIRS
+    square = jnp.concatenate(
+        [merged.reshape(wide_rows, L)[...], jnp.zeros((L - wide_rows, L), F32)], axis=0
+    ).T
+    col = lax.broadcasted_iota(jnp.int32, (rest, L), 1)
+    fourth = ((col >= some) & (col < G * B)) | ((col >= G * B + some) & (col < 2 * G * B))
+    for n in range(G - 1):
+        moved = pltpu.roll(square[span:], (G - 1 - n) * B, 1)
+        rows = square[n * rest : (n + 1) * rest] + jnp.where(fourth, moved, 0.0)
+        turned.at[pl.ds(n * rest // 4, rest // 4)].reshape(rest, L)[...] = rows
+    for d in (4, 3, 5, 2, 6, 1, 7):
         zz = lax.rem(z + d, Z)
-        rise = pltpu.make_async_remote_copy(
+        pltpu.make_async_remote_copy(
             src_ref=turned.at[pl.ds(3 * zz, 3)],
             dst_ref=z_got.at[d],
             send_sem=z_send,
             recv_sem=z_recv,
             device_id=(pair, zz * G + g),
             device_id_type=MESH,
-        )
-        rise.start()
-    stay = pltpu.make_async_copy(turned.at[pl.ds(3 * z, 3)], z_got.at[0], local.at[7])
+        ).start()
+    stay = pltpu.make_async_copy(turned.at[pl.ds(3 * z, 3)], z_got.at[0], local.at[8])
     stay.start()
     stay.wait()
     others = z_got.at[pl.ds(1, Z - 1)]
@@ -411,14 +445,15 @@
 def shards(phi, eigvecs, freqs, occupations, smearing, probes, pair_index):
     vmem = pl.BlockSpec(memory_space=pltpu.VMEM)
     hbm = pl.BlockSpec(memory_space=pl.ANY)
-    smem = pl.BlockSpec(memory_space=pltpu.SMEM)
     dma = pltpu.SemaphoreType.DMA
     return pl.pallas_call(
         kernel,
-        out_shape=jax.ShapeDtypeStruct((B, 2, M // PAIRS), F32),
-        in_specs=[smem, smem] + [hbm] * 5,
+        out_shape=pltpu.VMEM((B, 2, M // PAIRS), F32),
+        in_specs=[hbm] * 7,
         out_specs=vmem,
         scratch_shapes=[
+            pltpu.SMEM(pair_index.shape, jnp.int32),
+            pltpu.SMEM(probes.shape, F32),
             pltpu.VMEM((B, M, M), BF16),
             pltpu.VMEM(eigvecs.shape, BF16),
             pltpu.VMEM(freqs.shape, F32),
@@ -426,7 +461,7 @@
             pltpu.VMEM(freqs.shape, F32),
             pltpu.VMEM((NB, M * 4, L), F32),
             pltpu.VMEM((3, Z * G, B, 4, L), BF16),
-            pltpu.VMEM((2 * M, 2 * L), BF16),
+            pltpu.VMEM((2, M, 2 * L), BF16),
             pltpu.VMEM((G, L, 2 * L), BF16),
             pltpu.VMEM((M, M), BF16),
             pltpu.VMEM((M, M), BF16),
@@ -436,11 +471,12 @@
             pltpu.VMEM((NB, B, M // 4, 4, L), BF16),
             pltpu.VMEM((2, B, 1, M), F32),
             pltpu.VMEM((G, 2 * M, L), F32),
-            pltpu.VMEM((2, 2 * M // 4, 4, L), BF16),
-            pltpu.VMEM((2, 2 * M // 4, 4, L), BF16),
-            pltpu.VMEM((2, 2, G, Z, 3, 4, L), BF16),
-            pltpu.VMEM((PLANE + 1, 2, G, 3, 4, L), BF16),
-            pltpu.VMEM((L // 4, 4, L), F32),
+            pltpu.VMEM((2, 2, M // 4, 4, L), BF16),
+            pltpu.VMEM((2, 2, M // 4, 4, L), BF16),
+            pltpu.VMEM((2, 2, G - 1, Z, 3, 4, L), BF16),
+            pltpu.VMEM((PLANE + 1, 2, G - 1, 3, 4, L), BF16),
+            pltpu.VMEM((2, G, 3, 4, L), F32),
+            pltpu.VMEM((M // G // 4, 4, L), F32),
             pltpu.VMEM((Z, 3, 4, L), F32),
             dma((NP,)),
             dma((NP,)),
@@ -450,8 +486,8 @@
             dma,
             dma,
             dma,
-            dma((8,)),
-            dma((B // 2 + 4,)),
+            dma((9,)),
+            dma((B // 2 + 6,)),
         ],
         compiler_params=pltpu.CompilerParams(
             collective_id=0, has_side_effects=True, vmem_limit_bytes=60 * 1024 * 1024

time: 107 us -> 103 us (0.963)
  Pallas kernels: 106 us -> 102 us
    pallas_call x1, Pallas kernels: 106 us -> 102 us  [shards(): pl.pallas_call(kernel, out_shape=pltpu.VMEM((B, 2, M // PAIRS), F32), in_...]
where the time goes in v4:
time: 103 us
  Pallas kernels  102 us (99%)
    pallas_call x1, Pallas kernels, shards(): pl.pallas_call(kernel, out_shape=pltpu.VMEM((B, 2, M // PAIRS), F32), in_...  102 us

profile of v4, /device:TPU:8, one launch (start us, length us, event | category | flops | bytes accessed | tf_op | source)
XLA Modules:
  0.0 102.8 jit_solution(8955047964214377865)
XLA Ops:
  0.0 102.1 %sigma.1 = f32[12,2,48]{2,1,0:T(2,128)S(1)} custom-call(s32[1,3]{1,0:T(1,128)} %pidx_hbm.1, f32[1,2]{1,0:T(1,128)} %probes_hbm.1, bf16[1,12,384,384]{3,2,1,0:T(8,128)(2,1)} %phi_hbm.1, bf16[12,384,384]{2,1,0:T(8,128)(2,1)} %eig_hbm.1, f32[12,384]{1,0:T(8,128)} %freqs_hbm.1, f32[12,384]{1,0:T(8,128)} %occ_hbm.1, f32[12,384]{1,0:T(8,128)} %smear_hbm.1), custom_call_target="tpu_custom_call" | custom-call | tf_op jit(solution)/shard_map/sigma/pallas_call | solution.py:449
  102.1 0.6 copy.9

commit v5 on v4

--- a/solution.py
+++ b/solution.py
@@ -23,6 +23,7 @@
 PLANE = 15
 PIECES = ((0, 0, 12), (1, 0, 12), (2, 0, 6), (2, 6, 4), (2, 10, 2))
 NP = len(PIECES)
+ORDER = (1, 3, 0, 2)
 HOPS = (10, 9, 11, 6, 14, 8, 5, 7, 13, 15, 2, 4, 12, 1, 3)
 
 
@@ -189,8 +190,8 @@
 
     def ship_all(piece, t):
         zz = far(t)
-        for e in range(G):
-            ship(piece, zz, mate(e)).start()
+        for gg in ORDER:
+            ship(piece, zz, gg).start()
 
     def ship_near(piece):
         for e in range(1, G):
@@ -204,8 +205,8 @@
         def step_first(t, carry, group=group):
             zz = far(t)
             first_group(group, zz)
-            for e in range(G):
-                ship_first(group, zz, mate(e)).start()
+            for gg in ORDER:
+                ship_first(group, zz, gg).start()
             return carry
 
         lax.fori_loop(0, Z - 1, step_first, 0)
@@ -341,15 +342,13 @@
         )
         swap.start()
         swaps.append(swap)
+    spare = lax.broadcasted_iota(jnp.int32, (span, L), 1) >= span
+    rest = L - span
+    kept = []
     for w in range(2):
         part = last_lanes(core, w)
         for s in range(2):
             acc[2 * s + core, w * M : (w + 1) * M] += part[:, s * L : (s + 1) * L]
-
-    spare = lax.broadcasted_iota(jnp.int32, (span, L), 1) >= span
-    rest = L - span
-    kept = []
-    for w in range(2):
         swaps[w].wait_recv()
         for s in range(2):
             got = half_got.at[w, s].reshape(M, L)[...].astype(F32)

time: 103 us -> 104 us (level); the launches traced: 103 us -> 103 us
  no operation moved by 1% of the time
where the time goes in v5:
time: 104 us; the launch traced here: 103 us
  Pallas kernels  102 us (98%)
    pallas_call x1, Pallas kernels, shards(): pl.pallas_call(kernel, out_shape=pltpu.VMEM((B, 2, M // PAIRS), F32), in_...  102 us

profile of v5, /device:TPU:8, one launch (start us, length us, event | category | flops | bytes accessed | tf_op | source)
XLA Modules:
  0.0 102.7 jit_solution(275588451209800533)
XLA Ops:
  0.0 102.1 %sigma.1 = f32[12,2,48]{2,1,0:T(2,128)S(1)} custom-call(s32[1,3]{1,0:T(1,128)} %pidx_hbm.1, f32[1,2]{1,0:T(1,128)} %probes_hbm.1, bf16[1,12,384,384]{3,2,1,0:T(8,128)(2,1)} %phi_hbm.1, bf16[12,384,384]{2,1,0:T(8,128)(2,1)} %eig_hbm.1, f32[12,384]{1,0:T(8,128)} %freqs_hbm.1, f32[12,384]{1,0:T(8,128)} %occ_hbm.1, f32[12,384]{1,0:T(8,128)} %smear_hbm.1), custom_call_target="tpu_custom_call" | custom-call | tf_op jit(solution)/shard_map/sigma/pallas_call | solution.py:448
  102.1 0.6 copy.9
